TPU v7x, 128 devices: a whole 4x4x4 slice. The times are simulated.
128 devices in a mesh: seq: 32 (over x, y, core), chan: 4 (over z).
Axes of the slice: x: 4, y: 4, z: 4, core: 2. Of those that a mesh axis runs over, the one named last changes fastest.
Arguments:
- tokens: bfloat16 [16384, 8192], P('seq'), may hold values from -6 to 6
- proj_weight: bfloat16 [8192, 3, 2048], P('seq', None, 'chan'), may hold values from -0.0625 to 0.0625
- residues: float32 [16, 2048], P(None, 'chan'), may hold values from -1.5 to 1.5
- decay_rates: float32 [16, 2048], P(None, 'chan'), may hold values from 3.0517578e-05 to 0.05
- skip_gain: float32 [2048], P('chan'), may hold values from -3 to 3
- grad_out: bfloat16 [16384, 2048], P('seq', 'chan'), may hold values from -6 to 6
Outputs:
- gated_output: bfloat16 [16384, 2048], P('seq', 'chan')
- grad_tokens: bfloat16 [16384, 8192], P('seq', 'chan')
All inputs are finite; a program needn't handle non-finite values.
Results may differ from a plain program's by a relative error of at most 0.022.
Values may be sent and summed in bfloat16 or wider, within the bound.
A program may use at most 128 MiB of HBM per device.

v0:
```python
import math
import jax
import jax.numpy as jnp
from jax import lax
from jax.sharding import PartitionSpec as P

f32 = jnp.float32
bf16 = jnp.bfloat16


def dft_tables(block_len, flip=False):
    n_len = 2 * block_len
    k = jnp.arange(block_len, dtype=jnp.int32)[:, None]
    n = jnp.arange(block_len, dtype=jnp.int32)[None, :]
    if flip:
        n = block_len - 1 - n
    phase = k * n % n_len
    angle = 2.0 * math.pi / n_len * phase.astype(f32)
    cos_rows = jnp.cos(angle)
    sin_rows = jnp.sin(angle)
    nyquist = jnp.where(n % 2 == 0, 1.0, -1.0).astype(f32)
    sin_rows = jnp.where(k == 0, nyquist, sin_rows)
    fwd = jnp.concatenate([cos_rows, sin_rows], axis=0)
    weight = jnp.where(k == 0, 1.0, 2.0).astype(f32) / n_len
    inv = jnp.concatenate([cos_rows * weight, sin_rows * weight], axis=0).T
    return (fwd, inv)


def spectral_conv(signal, fwd, inv, h_a, h_a2, h_b):
    block_len = signal.shape[0]
    spec = jnp.dot(fwd, signal.astype(bf16), preferred_element_type=f32)
    xc = spec[:block_len]
    xs = spec[block_len:]
    pr = xc * h_a - xs * h_b
    pi = xc * h_b + xs * h_a2
    prod = jnp.concatenate([pr, pi], axis=0).astype(bf16)
    return jnp.dot(inv, prod, preferred_element_type=f32)


def local(tokens, proj_weight, residues, decay_rates, skip_gain, grad_out):
    tok_rows = tokens.shape[0]
    chan_count = skip_gain.shape[0]
    seq_count = lax.axis_size(SEQ)
    me = lax.axis_index(SEQ)
    flat_w = proj_weight.reshape(proj_weight.shape[0], 3 * chan_count)
    half = 3 * chan_count // 2
    pair_w = lax.all_gather(flat_w, "core", axis=0, tiled=True)
    mine_w = lax.dynamic_slice_in_dim(pair_w, lax.axis_index("core") * half, half, axis=1)
    plane_w = lax.all_gather(mine_w, "xy", axis=0, tiled=True)
    whole_w = lax.all_gather(plane_w, "core", axis=1, tiled=True)
    projected = jnp.dot(tokens, whole_w, preferred_element_type=f32)
    proj_vals = (
        lax.optimization_barrier(projected.astype(bf16))
        .astype(f32)
        .reshape(tok_rows, 3, chan_count)
    )
    query_in = proj_vals[:, 0]
    key_in = proj_vals[:, 1]
    value_in = proj_vals[:, 2]
    mixed_in = key_in * value_in
    grad_gate = grad_out.astype(f32)
    grad_mix = grad_gate * query_in
    rates = decay_rates
    mode_gain = residues * jnp.sqrt(-jnp.expm1(-2.0 * rates))
    steps = jnp.arange(tok_rows, dtype=f32)
    fwd_w = jnp.exp(-rates[:, None, :] * (tok_rows - 1 - steps)[None, :, None])
    bwd_w = jnp.exp(-rates[:, None, :] * steps[None, :, None])
    end_fwd = jnp.sum(fwd_w * mixed_in[None], axis=1)
    end_bwd = jnp.sum(bwd_w * grad_mix[None], axis=1)
    states = jnp.stack([end_fwd, end_bwd])
    every = lax.all_gather(states, SEQ)
    others = jnp.arange(seq_count, dtype=jnp.int32)
    gap_f = me - 1 - others
    gap_b = others - me - 1
    span = rates[None] * float(tok_rows)
    w_f = jnp.where(
        (gap_f >= 0)[:, None, None],
        jnp.exp(-span * jnp.maximum(gap_f, 0).astype(f32)[:, None, None]),
        0.0,
    )
    w_b = jnp.where(
        (gap_b >= 0)[:, None, None],
        jnp.exp(-span * jnp.maximum(gap_b, 0).astype(f32)[:, None, None]),
        0.0,
    )
    into_f = jnp.sum(w_f * every[:, 0], axis=0) * mode_gain
    into_b = jnp.sum(w_b * every[:, 1], axis=0) * mode_gain
    taps = jnp.sum(mode_gain[:, None, :] * bwd_w, axis=0)
    fwd, inv = dft_tables(tok_rows)
    fwd_b = fwd.astype(bf16)
    inv_b = inv.astype(bf16)
    fwd_r, inv_r = dft_tables(tok_rows, flip=True)
    spec = jnp.dot(fwd, taps, precision=lax.Precision.HIGHEST)
    row0 = (jnp.arange(tok_rows) == 0)[:, None]
    h_a = spec[:tok_rows]
    h_a2 = jnp.where(row0, spec[tok_rows : tok_rows + 1], h_a)
    h_b = jnp.where(row0, 0.0, spec[tok_rows:])
    local_f = spectral_conv(mixed_in, fwd_b, inv_b, h_a, h_a2, h_b)
    carry_f = jnp.sum(
        into_f[:, None, :] * jnp.exp(-rates[:, None, :] * (steps + 1.0)[None, :, None]), axis=0
    )
    filtered = local_f + carry_f + skip_gain[None, :] * mixed_in
    gated_output = (query_in * filtered).astype(bf16)
    grad_query = grad_gate * filtered
    local_b = spectral_conv(grad_mix, fwd_r.astype(bf16), inv_r.astype(bf16), h_a, h_a2, h_b)
    carry_b = jnp.sum(
        into_b[:, None, :] * jnp.exp(-rates[:, None, :] * (tok_rows - steps)[None, :, None]), axis=0
    )
    grad_conv = local_b + carry_b + skip_gain[None, :] * grad_mix
    grad_proj = jnp.stack([grad_query, grad_conv * value_in, grad_conv * key_in], axis=1).astype(
        bf16
    )
    grad_proj = grad_proj.reshape(tok_rows, 3 * chan_count)
    contract = (((1,), (1,)), ((), ()))
    dx_terms = lax.dot_general(grad_proj, whole_w, contract, preferred_element_type=f32)
    grad_tokens = lax.psum_scatter(dx_terms.astype(bf16), "chan", scatter_dimension=1, tiled=True)
    return (gated_output, grad_tokens)


SEQ = ("xy", "core")


def solution(mesh):
    cores = 2
    split = jax.sharding.Mesh(
        mesh.devices.reshape(mesh.shape["seq"] // cores, cores, mesh.shape["chan"]),
        ("xy", "core", "chan"),
    )
    placed = (
        P(SEQ, None),
        P(SEQ, None, "chan"),
        P(None, "chan"),
        P(None, "chan"),
        P("chan"),
        P(SEQ, "chan"),
    )
    return jax.shard_map(
        local,
        mesh=split,
        in_specs=placed,
        out_specs=(P(SEQ, "chan"), P(SEQ, "chan")),
        check_vma=False,
    )
```

profile of v0, /device:TPU:1, one launch (start us, length us, event | category | flops | bytes accessed | tf_op | source)
XLA Modules:
  0.0 390.3 jit_solution(8192776830825825899)
XLA Ops:
  7.2 2.3 copy.24
  9.6 16.7 %all-gather.6.cloned.1.call-done = bf16[512,1536]{0,1:T(8,128)(2,1)} async-done(((bf16[256,1536]{0,1:T(8,128)(2,1)}), bf16[512,1536]{0,1:T(8,128)(2,1)}) %all-gather.6.cloned.1.call-update) | async-done | bytes 1572880 | tf_op jit(solution)/shard_map/all_gather | solution.py:47
  26.3 2.1 constant_dynamic-slice_fusion
  28.4 100.2 %all-gather.8.cloned.1.call-done = bf16[8192,768]{0,1:T(8,128)(2,1)} async-done(((bf16[512,768]{0,1:T(8,128)(2,1)}), bf16[8192,768]{0,1:T(8,128)(2,1)}) %all-gather.8.cloned.1.call-update) | async-done | bytes 12582928 | tf_op jit(solution)/shard_map/all_gather | solution.py:49
  130.6 43.3 %all-gather.10.cloned.1.call-done = bf16[8192,1536]{0,1:T(8,128)(2,1)} async-done(((bf16[8192,768]{0,1:T(8,128)(2,1)}), bf16[8192,1536]{0,1:T(8,128)(2,1)}) %all-gather.10.cloned.1.call-update) | async-done | bytes 25165840 | tf_op jit(solution)/shard_map/all_gather | solution.py:50
  174.0 19.4 %fusion = bf16[512,1536]{0,1:T(8,128)(2,1)S(1)} fusion(bf16[8192,1536]{0,1:T(8,128)(2,1)} %all-gather.10.cloned.1.call-done, bf16[512,8192]{1,0:T(8,128)(2,1)} %param.6), kind=kOutput, calls=%fused_computation.8 | convolution fusion | flops 12885688320 | bytes 35127296 | tf_op jit(solution)/shard_map/dot_general | solution.py:51
  194.4 1.8 convert_multiply_fusion.1
  196.1 2.6 copy.27
  198.8 2.5 copy.25
  201.3 7.2 %multiply_reduce_fusion.3 = (f32[16,512]{1,0:T(8,128)S(1)}, f32[16,512]{1,0:T(8,128)S(1)}) fusion(f32[512,512]{1,0:T(8,128)} %copy.25, f32[512]{0:T(512)S(1)} %iota_subtract_fusion.2, f32[16,512]{1,0:T(8,128)S(1)} %get-tuple-element.32, f32[512,512]{1,0:T(8,128)} %copy.27), kind=kLoop, calls=%fused_computation.3 | loop fusion | flops 25149440 | bytes 2197504 | tf_op jit(solution)/shard_map/reduce_sum | solution.py:68
  209.5 3.8 fusion.48
  213.3 4.1 %fusion.41 = bf16[512,512]{1,0:T(8,128)(2,1)S(1)} fusion(f32[512]{0:T(512)S(1)} %fusion.57, s32[512]{0:T(512)S(1)} %iota_subtract_fusion.1, pred[512]{0:T(512)(128)(4,1)S(1)} %iota_compare_fusion), kind=kLoop, calls=%fused_computation.79 | loop fusion | flops 3932160 | bytes 528896 | tf_op jit(solution)/shard_map/convert.10
  217.4 9.7 %multiply_convert_fusion.3 = (bf16[512,512]{1,0:T(8,128)(2,1)}, bf16[512,512]{1,0:T(8,128)(2,1)}, bf16[512,512]{1,0:T(8,128)(2,1)}, f32[512,512]{1,0:T(8,128)S(1...) fusion(f32[512]{0:T(512)S(1)} %get-tuple-element.41, s32[512]{0:T(512)S(1)} %iota_subtract_fusion.1, ...), kind=kLoop, calls=%fused_computation.65 | loop fusion | flops 10223616 | bytes 3678720 | tf_op jit(solution)/shard_map/convert.11
  227.2 2.1 fusion.12
  229.2 2.1 fusion.27
  231.4 22.9 %all-gather.12.cloned.1.call-done = f32[64,16,512]{2,1,0:T(8,128)} async-done(((f32[2,16,512]{2,1,0:T(8,128)}), f32[64,16,512]{2,1,0:T(8,128)}) %all-gather.12.cloned.1.call-update) | async-done | bytes 2097168 | tf_op jit(solution)/shard_map/all_gather | solution.py:71
  254.3 2.1 fusion.15
  256.4 10.7 %multiply_reduce_fusion = (f32[512,512]{1,0:T(8,128)}, f32[512,512]{1,0:T(8,128)}, f32[512,512]{1,0:T(8,128)}) fusion(f32[512]{0:T(512)S(1)} %get-tuple-element.39, f32[16,512]{1,0:T(8,128)S(1)} %mul.373, f32[16,512]{1,0:T(8,128)S(1)} %get-tuple-element.32, f32[512]{0:T(512)S(1)} %get-tuple-element.40, f32[16,512]{1,0:T(8,128)S(1)} %get-tuple-element.17, ...), kind=kLoop, calls=%fused_computation | loop fusion | flops 36962304 | bytes 3280896 | tf_op jit(solution)/shard_map/reduce_sum | solution.py:106
  267.1 2.6 copy.30
  269.7 2.5 copy.29
  272.2 5.4 %fusion.1 = f32[1024,512]{1,0:T(8,128)S(1)} fusion(f32[512,512]{1,0:T(8,128)} %get-tuple-element.14, f32[512,512]{1,0:T(8,128)} %copy-done.3, f32[512,512]{1,0:T(8,128)} %copy-done.2), kind=kOutput, calls=%fused_computation.10 | convolution fusion | flops 3221749760 | bytes 5242880 | tf_op jit(solution)/shard_map/dot_general | solution.py:93
  281.5 1.8 fusion.42
  283.5 20.5 %convolution_convert_fusion = bf16[512,8192]{1,0:T(8,128)(2,1)} fusion(bf16[512,1536]{0,1:T(8,128)(2,1)S(1)} %bitcast.59, bf16[8192,1536]{0,1:T(8,128)(2,1)} %all-gather.10.cloned.1.call-done), kind=kOutput, calls=%fused_computation.6 | convolution fusion | flops 12889096192 | bytes 35127296 | tf_op jit(solution)/shard_map/dot_general | solution.py:115
  306.1 77.8 %reduce-scatter.2.cloned.1.call-done = bf16[512,2048]{1,0:T(8,128)(2,1)} async-done(((bf16[512,8192]{1,0:T(8,128)(2,1)}), bf16[512,2048]{1,0:T(8,128)(2,1)}) %reduce-scatter.2.cloned.1.call-update) | async-done | bytes 2097168 | tf_op jit(solution)/shard_map/reduce_scatter | solution.py:116
  (73 shorter events, 10.2 us)
Async XLA Ops:
  7.2 19.1 %all-gather.6.cloned.1.call-start = ((), (), s32[]{:S(2)}) async-start(), calls=%async_computation.1 | async-start | bytes 2359296 | tf_op jit(solution)/shard_map/all_gather | solution.py:47
  9.5 119.0 %all-gather.8.cloned.1.call-start = ((), (), s32[]{:S(2)}) async-start(), calls=%async_computation.2 | async-start | bytes 13369344 | tf_op jit(solution)/shard_map/all_gather | solution.py:49
  28.3 145.6 %all-gather.10.cloned.1.call-start = ((), (), s32[]{:S(2)}) async-start(), calls=%async_computation.3 | async-start | bytes 37748736 | tf_op jit(solution)/shard_map/all_gather | solution.py:50
  128.6 2.1 copy-start.18
  128.6 125.7 %all-gather.12.cloned.1.call-start = ((), (), s32[]{:S(2)}) async-start(), calls=%async_computation.5 | async-start | bytes 2162688 | tf_op jit(solution)/shard_map/all_gather | solution.py:71
  193.3 1.0 copy-start.8
  209.1 174.7 %reduce-scatter.2.cloned.1.call-start = ((), (), s32[]{:S(2)}) async-start(), calls=%async_computation.4 | async-start | bytes 10485760 | tf_op jit(solution)/shard_map/reduce_scatter | solution.py:116
  213.3 13.9 %copy-start.2 = (f32[512,512]{1,0:T(8,128)}, f32[512,512]{1,0:T(8,128)S(1)}, u32[]{:S(2)}) copy-start(f32[512,512]{1,0:T(8,128)S(1)} %fusion.48) | copy-start | bytes 3145732
  213.3 13.9 %copy-start = (f32[512,512]{0,1:T(8,128)S(1)}, f32[512,512]{0,1:T(8,128)}, u32[]{:S(2)}) copy-start(f32[512,512]{0,1:T(8,128)} %get-tuple-element.27) | copy-start | bytes 3145732
  227.1 2.1 copy-start.3
  227.2 2.1 copy-start.4
  231.4 25.0 %copy-start.19 = (f32[16,512]{1,0:T(8,128)S(1)}, f32[16,512]{1,0:T(8,128)}, u32[]{:S(2)}) copy-start(f32[16,512]{1,0:T(8,128)} %param.8) | copy-start | bytes 98308
  272.2 5.5 %copy-start.6 = (f32[1024,512]{1,0:T(8,128)S(1)}, f32[1024,512]{1,0:T(8,128)}, u32[]{:S(2)}) copy-start(f32[1024,512]{1,0:T(8,128)} %fusion.12) | copy-start | bytes 6291460
  272.2 5.5 %copy-start.7 = (f32[1024,512]{1,0:T(8,128)S(1)}, f32[1024,512]{1,0:T(8,128)}, u32[]{:S(2)}) copy-start(f32[1024,512]{1,0:T(8,128)} %fusion.27) | copy-start | bytes 6291460
  277.7 1.2 copy-start.5
  277.7 1.5 copy-start.14
  277.7 1.7 copy-start.16
  277.7 1.8 copy-start.17
  277.7 1.8 copy-start.20
  279.5 1.2 copy-start.1
  279.5 1.4 copy-start.9
  279.5 1.7 copy-start.10
  279.5 1.8 copy-start.12
  279.6 2.0 copy-start.13
  (2 other events, 2.1 us)
Sparse Core Ops, SparseCore 0:
  10.2 15.9 all-gather.5
  28.9 99.5 all-gather.7
  130.2 43.7 all-gather.9
  209.2 45.0 all-gather.11
  304.2 79.6 reduce-scatter.1
where the time goes:
time: 391 us; the launch traced here: 390 us
  waiting for transfers between devices  261 us (67%)
  matrix products  52.1 us (13%)
  other arithmetic  41.3 us (11%)
  local copies, waits for them, and re-layouts  21.6 us (6%)
  between operations  14.1 us (4%)
    all_gather x1, waiting for transfers between devices, local(): plane_w = lax.all_gather(mine_w, 'xy', axis=0, tiled=True)  100 us
    reduce_scatter x1, waiting for transfers between devices, local(): lax.psum_scatter(dx_terms.astype(bf16), 'chan', scatter_dimension=1, tile...  77.8 us
    all_gather x1, waiting for transfers between devices, local(): whole_w = lax.all_gather(plane_w, 'core', axis=1, tiled=True)  43.3 us
    all_gather x1, waiting for transfers between devices, local(): every = lax.all_gather(states, SEQ)  22.9 us
    dot_general x1, matrix products, local(): lax.dot_general(grad_proj, whole_w, contract, preferred_element_type=f32)  20.5 us
    dot_general x1, matrix products, local(): projected = jnp.dot(tokens, whole_w, preferred_element_type=f32)  19.4 us
    all_gather x1, waiting for transfers between devices, local(): pair_w = lax.all_gather(flat_w, 'core', axis=0, tiled=True)  16.7 us
    another operation x3, other arithmetic  14.4 us
  transfers between devices with their start and end apart: 5, of which 5 were waited for; matrix products, arithmetic and copies ran while one was open for 6% of the time, Pallas kernels for 0%

commit v1 on v0

--- a/solution.py
+++ b/solution.py
@@ -44,7 +44,9 @@
     me = lax.axis_index(SEQ)
     flat_w = proj_weight.reshape(proj_weight.shape[0], 3 * chan_count)
     half = 3 * chan_count // 2
-    pair_w = lax.all_gather(flat_w, "core", axis=0, tiled=True)
+    pair_w = jnp.concatenate(
+        lax.all_to_all(jnp.stack([flat_w] * lax.axis_size("core")), "core", 0, 0), axis=0
+    )
     mine_w = lax.dynamic_slice_in_dim(pair_w, lax.axis_index("core") * half, half, axis=1)
     plane_w = lax.all_gather(mine_w, "xy", axis=0, tiled=True)
     whole_w = lax.all_gather(plane_w, "core", axis=1, tiled=True)

time: 391 us -> 374 us (0.957)
  waiting for transfers between devices: 261 us -> 240 us
  starting transfers between devices: 0.38 us -> 5.39 us
    all_gather x1 -> x0, waiting for transfers between devices: 16.7 us -> none  [local(): pair_w = lax.all_gather(flat_w, 'core', axis=0, tiled=True)]
    all_gather x1, waiting for transfers between devices: 100 us -> 92.1 us  [local(): plane_w = lax.all_gather(mine_w, 'xy', axis=0, tiled=True)]
    all_to_all x0 -> x1, starting transfers between devices: none -> 5.08 us  [local(): lax.all_to_all(jnp.stack([flat_w] * lax.axis_size('core')), 'core', 0, 0)]
    another operation x3 -> x4, other arithmetic: 14.4 us -> 15.7 us
where the time goes in v1:
time: 374 us; the launch traced here: 373 us
  waiting for transfers between devices  240 us (64%)
  matrix products  50.7 us (14%)
  other arithmetic  42.6 us (11%)
  local copies, waits for them, and re-layouts  20.3 us (5%)
  between operations  14.1 us (4%)
  starting transfers between devices  5.39 us (1%)
    all_gather x1, waiting for transfers between devices, local(): plane_w = lax.all_gather(mine_w, 'xy', axis=0, tiled=True)  92.1 us
    reduce_scatter x1, waiting for transfers between devices, local(): lax.psum_scatter(dx_terms.astype(bf16), 'chan', scatter_dimension=1, tile...  77.8 us
    all_gather x1, waiting for transfers between devices, local(): whole_w = lax.all_gather(plane_w, 'core', axis=1, tiled=True)  45 us
    all_gather x1, waiting for transfers between devices, local(): every = lax.all_gather(states, SEQ)  22.9 us
    dot_general x1, matrix products, local(): projected = jnp.dot(tokens, whole_w, preferred_element_type=f32)  19.5 us
    dot_general x1, matrix products, local(): lax.dot_general(grad_proj, whole_w, contract, preferred_element_type=f32)  19.1 us
    another operation x3, other arithmetic  14.5 us
    reduce_sum x1, other arithmetic, local(): jnp.sum(into_b[:, None, :] * jnp.exp(-rates[:, None, :] * (tok_rows - ste...  10.7 us
  transfers between devices with their start and end apart: 5, of which 5 were waited for; matrix products, arithmetic and copies ran while one was open for 6% of the time, Pallas kernels for 0%

profile of v1, /device:TPU:1, one launch (start us, length us, event | category | flops | bytes accessed | tf_op | source)
XLA Modules:
  0.0 373.1 jit_solution(530419900369070687)
XLA Ops:
  7.2 1.4 copy.32
  9.9 5.1 %all-to-all-start = ((bf16[2,256,1536]{1,2,0:T(8,128)(2,1)}), bf16[2,256,1536]{1,2,0:T(8,128)(2,1)S(1)}, u32[]{:S(2)}, u32[]{:S(2)}) async-start(bf16[2,256,1536]{1,2,0:T(8,128)(2,1)} %pad_maximum_fusion.2), calls=%async_computation | async-start | bytes 3145728 | tf_op jit(solution)/shard_map/all_to_all | solution.py:48
  14.9 2.1 all-to-all-done
  18.8 92.1 %all-gather.5.cloned.1.call-done = bf16[8192,768]{1,0:T(8,128)(2,1)} async-done(((bf16[512,768]{1,0:T(8,128)(2,1)}), bf16[8192,768]{1,0:T(8,128)(2,1)}) %all-gather.5.cloned.1.call-update) | async-done | bytes 12582928 | tf_op jit(solution)/shard_map/all_gather | solution.py:51
  113.0 45.0 %all-gather.7.cloned.1.call-done = bf16[8192,1536]{1,0:T(8,128)(2,1)} async-done(((bf16[8192,768]{1,0:T(8,128)(2,1)}), bf16[8192,1536]{1,0:T(8,128)(2,1)}) %all-gather.7.cloned.1.call-update) | async-done | bytes 25165840 | tf_op jit(solution)/shard_map/all_gather | solution.py:52
  158.0 19.5 %fusion = bf16[512,1536]{0,1:T(8,128)(2,1)S(1)} fusion(bf16[8192,1536]{1,0:T(8,128)(2,1)} %all-gather.7.cloned.1.call-done, bf16[512,8192]{1,0:T(8,128)(2,1)} %param.6), kind=kOutput, calls=%fused_computation.8 | convolution fusion | flops 12885688320 | bytes 35127296 | tf_op jit(solution)/shard_map/dot_general | solution.py:53
  178.5 1.8 convert_multiply_fusion.1
  180.3 2.6 copy.36
  182.9 2.5 copy.34
  185.4 7.2 %multiply_reduce_fusion.3 = (f32[16,512]{1,0:T(8,128)S(1)}, f32[16,512]{1,0:T(8,128)S(1)}) fusion(f32[512,512]{1,0:T(8,128)} %copy.34, f32[512]{0:T(512)S(1)} %iota_subtract_fusion.2, f32[16,512]{1,0:T(8,128)S(1)} %get-tuple-element.34, f32[512,512]{1,0:T(8,128)} %copy.36), kind=kLoop, calls=%fused_computation.3 | loop fusion | flops 25149440 | bytes 2197504 | tf_op jit(solution)/shard_map/reduce_sum | solution.py:70
  193.6 3.8 %fusion.48 = f32[512,512]{1,0:T(8,128)S(1)} fusion(), kind=kLoop, calls=%fused_computation.87 | loop fusion | flops 3670016 | bytes 1048576 | tf_op jit(solution)/shard_map/cos | solution.py:19
  197.4 4.1 %fusion.41 = bf16[512,512]{1,0:T(8,128)(2,1)S(1)} fusion(f32[512]{0:T(512)S(1)} %fusion.57, s32[512]{0:T(512)S(1)} %iota_subtract_fusion.1, pred[512]{0:T(512)(128)(4,1)S(1)} %iota_compare_fusion), kind=kLoop, calls=%fused_computation.80 | loop fusion | flops 3932160 | bytes 528896 | tf_op jit(solution)/shard_map/convert.10
  201.5 9.8 %multiply_convert_fusion.3 = (bf16[512,512]{1,0:T(8,128)(2,1)}, bf16[512,512]{1,0:T(8,128)(2,1)}, bf16[512,512]{1,0:T(8,128)(2,1)}, f32[512,512]{1,0:T(8,128)S(1...) fusion(f32[512]{0:T(512)S(1)} %get-tuple-element.43, s32[512]{0:T(512)S(1)} %iota_subtract_fusion.1, ...), kind=kLoop, calls=%fused_computation.66 | loop fusion | flops 10223616 | bytes 3678720 | tf_op jit(solution)/shard_map/convert.11
  211.3 2.1 fusion.12
  213.4 2.1 fusion.27
  215.5 22.9 %all-gather.9.cloned.1.call-done = f32[64,16,512]{2,1,0:T(8,128)} async-done(((f32[2,16,512]{2,1,0:T(8,128)}), f32[64,16,512]{2,1,0:T(8,128)}) %all-gather.9.cloned.1.call-update) | async-done | bytes 2097168 | tf_op jit(solution)/shard_map/all_gather | solution.py:73
  238.5 2.1 fusion.15
  240.6 10.7 %multiply_reduce_fusion = (f32[512,512]{1,0:T(8,128)}, f32[512,512]{1,0:T(8,128)}, f32[512,512]{1,0:T(8,128)}) fusion(f32[512]{0:T(512)S(1)} %get-tuple-element.41, f32[16,512]{1,0:T(8,128)S(1)} %mul.373, f32[16,512]{1,0:T(8,128)S(1)} %get-tuple-element.34, f32[512]{0:T(512)S(1)} %get-tuple-element.42, f32[16,512]{1,0:T(8,128)S(1)} %get-tuple-element.19, ...), kind=kLoop, calls=%fused_computation | loop fusion | flops 36962304 | bytes 3280896 | tf_op jit(solution)/shard_map/reduce_sum | solution.py:108
  251.3 2.6 copy.39
  253.8 2.5 copy.38
  256.4 5.4 %fusion.1 = f32[1024,512]{1,0:T(8,128)S(1)} fusion(f32[512,512]{1,0:T(8,128)} %get-tuple-element.16, f32[512,512]{1,0:T(8,128)} %copy-done.3, f32[512,512]{1,0:T(8,128)} %copy-done.2), kind=kOutput, calls=%fused_computation.10 | convolution fusion | flops 3221749760 | bytes 5242880 | tf_op jit(solution)/shard_map/dot_general | solution.py:95
  265.7 1.8 fusion.42
  267.6 19.1 %convolution_convert_fusion = bf16[512,8192]{1,0:T(8,128)(2,1)} fusion(bf16[512,1536]{0,1:T(8,128)(2,1)S(1)} %bitcast.61, bf16[8192,1536]{1,0:T(8,128)(2,1)} %all-gather.7.cloned.1.call-done), kind=kOutput, calls=%fused_computation.6 | convolution fusion | flops 12889096192 | bytes 35127296 | tf_op jit(solution)/shard_map/dot_general | solution.py:117
  288.8 77.8 %reduce-scatter.2.cloned.1.call-done = bf16[512,2048]{1,0:T(8,128)(2,1)} async-done(((bf16[512,8192]{1,0:T(8,128)(2,1)}), bf16[512,2048]{1,0:T(8,128)(2,1)}) %reduce-scatter.2.cloned.1.call-update) | async-done | bytes 2097168 | tf_op jit(solution)/shard_map/reduce_scatter | solution.py:118
  (74 shorter events, 13.0 us)
Async XLA Ops:
  9.9 7.2 %all-to-all-start = ((bf16[2,256,1536]{1,2,0:T(8,128)(2,1)}), bf16[2,256,1536]{1,2,0:T(8,128)(2,1)S(1)}, u32[]{:S(2)}, u32[]{:S(2)}) async-start(bf16[2,256,1536]{1,2,0:T(8,128)(2,1)} %pad_maximum_fusion.2), calls=%async_computation | async-start | bytes 3145728 | tf_op jit(solution)/shard_map/all_to_all | solution.py:48
  14.9 96.0 %all-gather.5.cloned.1.call-start = ((), (), s32[]{:S(2)}) async-start(), calls=%async_computation.2 | async-start | bytes 13369344 | tf_op jit(solution)/shard_map/all_gather | solution.py:51
  18.7 139.3 %all-gather.7.cloned.1.call-start = ((), (), s32[]{:S(2)}) async-start(), calls=%async_computation.3 | async-start | bytes 37748736 | tf_op jit(solution)/shard_map/all_gather | solution.py:52
  110.9 2.1 copy-start.18
  110.9 127.5 %all-gather.9.cloned.1.call-start = ((), (), s32[]{:S(2)}) async-start(), calls=%async_computation.5 | async-start | bytes 2162688 | tf_op jit(solution)/shard_map/all_gather | solution.py:73
  177.5 1.0 copy-start.8
  193.3 173.3 %reduce-scatter.2.cloned.1.call-start = ((), (), s32[]{:S(2)}) async-start(), calls=%async_computation.4 | async-start | bytes 10485760 | tf_op jit(solution)/shard_map/reduce_scatter | solution.py:118
  197.4 13.9 %copy-start.2 = (f32[512,512]{1,0:T(8,128)}, f32[512,512]{1,0:T(8,128)S(1)}, u32[]{:S(2)}) copy-start(f32[512,512]{1,0:T(8,128)S(1)} %fusion.48) | copy-start | bytes 3145732
  197.4 13.9 %copy-start = (f32[512,512]{0,1:T(8,128)S(1)}, f32[512,512]{0,1:T(8,128)}, u32[]{:S(2)}) copy-start(f32[512,512]{0,1:T(8,128)} %get-tuple-element.29) | copy-start | bytes 3145732
  211.3 2.1 copy-start.3
  211.3 2.1 copy-start.4
  215.5 25.0 %copy-start.19 = (f32[16,512]{1,0:T(8,128)S(1)}, f32[16,512]{1,0:T(8,128)}, u32[]{:S(2)}) copy-start(f32[16,512]{1,0:T(8,128)} %param.8) | copy-start | bytes 98308
  256.4 5.5 %copy-start.6 = (f32[1024,512]{1,0:T(8,128)S(1)}, f32[1024,512]{1,0:T(8,128)}, u32[]{:S(2)}) copy-start(f32[1024,512]{1,0:T(8,128)} %fusion.12) | copy-start | bytes 6291460
  256.4 5.5 %copy-start.7 = (f32[1024,512]{1,0:T(8,128)S(1)}, f32[1024,512]{1,0:T(8,128)}, u32[]{:S(2)}) copy-start(f32[1024,512]{1,0:T(8,128)} %fusion.27) | copy-start | bytes 6291460
  261.8 1.2 copy-start.5
  261.9 1.5 copy-start.14
  261.9 1.7 copy-start.16
  261.9 1.8 copy-start.17
  261.9 1.8 copy-start.20
  263.7 1.2 copy-start.1
  263.7 1.4 copy-start.9
  263.7 1.7 copy-start.10
  263.7 1.8 copy-start.12
  263.7 2.0 copy-start.13
  (2 other events, 2.1 us)
Sparse Core Ops, SparseCore 0:
  18.8 92.0 all-gather.4
  112.6 45.3 all-gather.6
  193.4 45.0 all-gather.8
  286.9 79.6 reduce-scatter.1
